TPU v7x, 32 devices: a whole 2x2x4 slice. The times are simulated.
32 devices in a mesh: groups: 2 (over y), seq: 4 (over z), dp: 4 (over x, core), head: 1.
Axes of the slice: x: 2, y: 2, z: 4, core: 2. Of those that a mesh axis runs over, the one named last changes fastest.
Arguments:
- x_in: bfloat16 [8, 2048, 768], P(('groups', 'dp'), 'seq'), parts along dimension 0, may hold values from -6 to 6
- kernel_weight: bfloat16 [3, 768, 1536], P(None, None, 'head'), may hold values from -0.125 to 0.125
- conv_bias: float32 [1536], P('head'), may hold values from -3 to 3
- norm_gain: float32 [1536], replicated, may hold values from 0.25 to 1.75
- w_query: bfloat16 [1536, 1024], P(None, 'head'), may hold values from -8 to 8
- w_key: bfloat16 [1536, 128], replicated, may hold values from -1 to 1
- w_value: bfloat16 [1536, 192], replicated, may hold values from -0.15625 to 0.15625
- w_out: bfloat16 [1536, 1536], P('head'), may hold values from -0.15625 to 0.15625
- cotangent: bfloat16 [8, 1024, 1536], P(('groups', 'dp'), 'seq'), parts along dimension 0, may hold values from -0.75 to 0.75
Outputs:
- mixed: bfloat16 [8, 1024, 1536], P(('groups', 'dp'), 'seq', 'head'), parts along dimension 0
- grad_out_t: float32 [3072, 1536], P(('groups', 'dp'), 'head'), parts along dimension 0
There are 2 independent parts, one for each index of `groups`. A program takes and returns all parts, laid end to end along the dimension named above; an argument that names none is the same for every part. Nothing has to cross between parts.
All inputs are finite; a program needn't handle non-finite values.
Results may differ from a plain program's by a relative error of at most 0.02.
Values may be sent and summed in bfloat16 or wider, within the bound.
A program may use at most 128 MiB of HBM per device.

v0:
```python
import math

import jax
import jax.numpy as jnp
from jax import lax
from jax.sharding import PartitionSpec as P

KEY = 128
VAL = 192
KERNEL_TAPS = 3
DILATION_STEP = 2


rope_base = 10000.0
norm_eps = 1e-06


def padded(cells, sides, width):
    for axis, dim in sides:
        count = lax.axis_size(axis)
        ends = count - 1
        head = lax.slice_in_dim(cells, 0, width, axis=dim)
        tail = lax.slice_in_dim(cells, cells.shape[dim] - width, cells.shape[dim], axis=dim)
        cells = jnp.concatenate(
            [
                lax.ppermute(tail, axis, [(i, (i + 1) % count) for i in range(ends)]),
                cells,
                lax.ppermute(head, axis, [((i + 1) % count, i) for i in range(ends)]),
            ],
            axis=dim,
        )
    return cells


def rotate(vectors, positions):
    halfway = vectors.shape[-1] // 2
    frequency = jnp.exp(
        -math.log(rope_base) * 2.0 * jnp.arange(halfway, dtype=jnp.float32) / vectors.shape[-1]
    )
    angles = positions.astype(jnp.float32)[:, None] * frequency[None, :]
    layout = (positions.shape[0],) + (1,) * (vectors.ndim - 2) + (halfway,)
    cosine = jnp.cos(angles).reshape(layout)
    sines = jnp.sin(angles).reshape(layout)
    leading = vectors[..., :halfway]
    trailing = vectors[..., halfway:]
    return jnp.concatenate(
        [leading * cosine - trailing * sines, leading * sines + trailing * cosine], axis=-1
    )


def attend_pieces(queries, key_rows, value_rows, state_in):
    total_keys = key_rows.shape[0]
    block_size = math.gcd(total_keys, 512)

    def one_block(block_index, state):
        running_max, running_sum, weighted = state
        key_block = lax.dynamic_slice_in_dim(key_rows, block_index * block_size, block_size, 0)
        value_block = lax.dynamic_slice_in_dim(value_rows, block_index * block_size, block_size, 0)
        scores = jnp.einsum(
            "thd,ud->htu", queries, key_block, preferred_element_type=jnp.float32
        ) * KEY ** (-0.5)
        new_max = jnp.maximum(running_max, jnp.max(scores, axis=-1))
        rescale = jnp.exp(running_max - new_max)
        weights = jnp.exp(scores - new_max[:, :, None])
        running_sum = running_sum * rescale + jnp.sum(weights, axis=-1)
        weighted = weighted * jnp.transpose(rescale)[:, :, None] + jnp.einsum(
            "htu,uv->thv",
            weights.astype(jnp.bfloat16),
            value_block,
            preferred_element_type=jnp.float32,
        )
        return (new_max, running_sum, weighted)

    return lax.fori_loop(0, total_keys // block_size, one_block, state_in)


def local(x_in, kernel_weight, conv_bias, norm_gain, w_query, w_key, w_value, w_out, cotangent):
    inputs = x_in[0]
    edge_padding = DILATION_STEP * (KERNEL_TAPS - 1) // 2
    padded_rows = padded(inputs, (("seq", 0),), edge_padding)
    padded_row_count = inputs.shape[0]
    before_activation = jnp.broadcast_to(
        conv_bias[None, :], (padded_row_count, kernel_weight.shape[2])
    )
    for kernel_tap_index in range(KERNEL_TAPS):
        before_activation = before_activation + jnp.dot(
            padded_rows[
                kernel_tap_index * DILATION_STEP : kernel_tap_index * DILATION_STEP
                + padded_row_count
            ],
            kernel_weight[kernel_tap_index],
            preferred_element_type=jnp.float32,
        )
    activated = jax.nn.gelu(before_activation)
    pooled = jnp.max(activated.reshape(padded_row_count // 2, 2, -1), axis=1).astype(jnp.bfloat16)
    token_count = pooled.shape[0]
    features = lax.all_gather(pooled, "head", axis=1, tiled=True)
    widened = features.astype(jnp.float32)
    squares = jnp.mean(widened * widened, axis=-1, keepdims=True)
    normed = (widened * lax.rsqrt(squares + norm_eps) * norm_gain).astype(jnp.bfloat16)
    seq_offset = lax.axis_index("seq") * token_count
    positions = seq_offset + jnp.arange(token_count, dtype=jnp.int32)
    local_heads = w_query.shape[1] // KEY
    queries = rotate(
        jnp.dot(normed, w_query, preferred_element_type=jnp.float32).reshape(
            token_count, local_heads, KEY
        ),
        positions,
    ).astype(jnp.bfloat16)
    own_rows = token_count // lax.axis_size("head")
    row_offset = lax.axis_index("head") * own_rows
    own_normed = lax.dynamic_slice_in_dim(normed, row_offset, own_rows, 0)
    own_positions = seq_offset + row_offset + jnp.arange(own_rows, dtype=jnp.int32)
    key_rows = rotate(
        jnp.dot(own_normed, w_key, preferred_element_type=jnp.float32), own_positions
    ).astype(jnp.bfloat16)
    value_rows = jnp.dot(own_normed, w_value, preferred_element_type=jnp.float32).astype(
        jnp.bfloat16
    )
    start_state = (
        jnp.full((local_heads, token_count), -1e30, jnp.float32),
        jnp.zeros((local_heads, token_count), jnp.float32),
        jnp.zeros((token_count, local_heads, VAL), jnp.float32),
    )
    final_state = attend_pieces(
        queries,
        lax.all_gather(key_rows, ("seq", "head"), axis=0, tiled=True),
        lax.all_gather(value_rows, ("seq", "head"), axis=0, tiled=True),
        start_state,
    )
    running_max, running_sum, weighted = final_state
    attended = (
        (weighted / jnp.transpose(running_sum)[:, :, None])
        .astype(jnp.bfloat16)
        .reshape(token_count, local_heads * VAL)
    )
    projected = lax.psum_scatter(
        lax.dot_general(
            w_out, attended, (((0,), (1,)), ((), ())), preferred_element_type=jnp.float32
        ).astype(jnp.bfloat16),
        "head",
        scatter_dimension=0,
        tiled=True,
    ).astype(jnp.float32)
    mixed = (pooled.astype(jnp.float32) + jnp.transpose(projected)).astype(jnp.bfloat16)[None]
    upstream = cotangent[0]
    dp_rows = upstream.shape[1] // lax.axis_size("dp")
    whole_grad = lax.dot_general(
        upstream, attended, (((0,), (0,)), ((), ())), preferred_element_type=jnp.float32
    )
    summed = lax.psum(whole_grad, ("seq", "dp"))
    gradient = lax.dynamic_slice_in_dim(summed, lax.axis_index("dp") * dp_rows, dp_rows, 0)
    return (mixed, gradient)


def solution(mesh):
    return jax.shard_map(
        local,
        mesh=mesh,
        in_specs=(
            P(("groups", "dp"), "seq", None),
            P(None, None, "head"),
            P("head"),
            P(),
            P(None, "head"),
            P(),
            P(),
            P("head", None),
            P(("groups", "dp"), "seq", None),
        ),
        out_specs=(P(("groups", "dp"), "seq", "head"), P(("groups", "dp"), "head")),
        check_vma=False,
    )
```

profile of v0, /device:TPU:0, one launch (start us, length us, event | category | flops | bytes accessed | tf_op | source)
XLA Modules:
  0.0 299.3 jit_solution(1337052279311216444)
XLA Ops:
  7.2 0.9 slice_bitcast_fusion
  8.1 1.4 collective-permute-start.1
  9.5 5.6 %collective-permute-start = (bf16[2,768]{1,0:T(2,128)(2,1)S(1)}, bf16[2,768]{1,0:T(2,128)(2,1)S(1)}, u32[]{:S(2)}, u32[]{:S(2)}) collective-permute-start(bf16[2,768]{1,0:T(2,128)(2,1)S(1)} %get-tuple-element.185), channel_id=1, source_target_pairs={{0,4},{4,8},{8,12},{1,5},{5,9},{9,13},{2,6},{6,10},{10,14},{3,7},{... | collective-permute-start | bytes 9224 | tf_op jit(solution)/shard_map/ppermute | solution.py:26
  15.1 5.0 %fusion.32 = f32[512,1536]{1,0:T(8,128)} fusion(bf16[3,768,1536]{2,1,0:T(8,128)(2,1)} %param.12, bf16[1,512,768]{2,1,0:T(8,128)(2,1)} %param.11), kind=kOutput, calls=%fused_computation.43 | convolution fusion | flops 1207959552 | bytes 6291456 | tf_op jit(solution)/shard_map/dot_general | solution.py:86
  20.1 4.3 %fusion.19 = f32[512,1536]{1,0:T(8,128)S(1)} fusion(f32[512,1536]{1,0:T(8,128)} %fusion.32, bf16[3,768,1536]{2,1,0:T(8,128)(2,1)} %param.12, f32[1536]{0:T(1024)S(1)} %copy-done.8, bf16[512,768]{1,0:T(8,128)(2,1)} %bitcast.80, bf16[2,768]{1,0:T(2,128)(2,1)S(1)} %collective-permute-done), kind=kOutput, calls=%fused_computation.27 | convolution fusion | flops 1211105280 | bytes 9446400 | tf_op jit(solution)/shard_map/dot_general | solution.py:86
  24.5 4.8 %fusion.26 = bf16[512,1536]{1,0:T(8,128)(2,1)} fusion(f32[512,1536]{1,0:T(8,128)S(1)} %fusion.19, bf16[3,768,1536]{2,1,0:T(8,128)(2,1)} %param.12, bf16[2,768]{1,0:T(2,128)(2,1)S(1)} %collective-permute-done.1, bf16[512,768]{1,0:T(8,128)(2,1)S(1)} %bitcast.81), kind=kOutput, calls=%fused_computation.34 | convolution fusion | flops 1217396736 | bytes 7867392 | tf_op jit(solution)/shard_map/dot_general | solution.py:86
  29.3 4.5 %reshape.92 = bf16[256,2,1536]{2,1,0:T(2,128)(2,1)} reshape(bf16[512,1536]{1,0:T(8,128)(2,1)} %fusion.26) | data formatting | bytes 3145728 | tf_op jit(solution)/shard_map/reshape | solution.py:95
  33.8 6.1 %reduce_max.22 = bf16[256,1536]{1,0:T(8,128)(2,1)} reduce(bf16[256,2,1536]{2,1,0:T(2,128)(2,1)} %reshape.92, bf16[]{:T(256)} %constant.148), dimensions={1}, to_apply=%region_0.0 | reduce | flops 393216 | bytes 2359298 | tf_op jit(solution)/shard_map/reduce_max | solution.py:95
  39.9 1.4 fusion.38
  41.3 2.4 convolution_convert_fusion.1
  43.7 1.7 fusion.50
  45.8 0.8 copy.13
  46.5 0.8 copy.15
  47.3 15.7 %all_gather.7 = bf16[1024,128]{0,1:T(8,128)(2,1)} all-gather(bf16[256,128]{0,1:T(8,128)(2,1)S(1)} %pad_maximum_fusion.5), channel_id=1, replica_groups=mesh['groups'=2,'seq'=4,'dp'=4,'head'=1] {'seq','head'}, dimensions={0}, use_global_device_ids=true | all-gather | bytes 327680 | tf_op jit(solution)/shard_map/all_gather | solution.py:127
  63.0 15.1 %all_gather.8 = bf16[1024,192]{0,1:T(8,128)(2,1)S(1)} all-gather(bf16[256,192]{0,1:T(8,128)(2,1)} %convolution_convert_fusion.1), channel_id=1, replica_groups=mesh['groups'=2,'seq'=4,'dp'=4,'head'=1] {'seq','head'}, dimensions={0}, use_global_device_ids=true | all-gather | bytes 491520 | tf_op jit(solution)/shard_map/all_gather | solution.py:128
  78.1 2.2 convolution_bitcast_fusion.1
  81.7 1.1 pad_maximum_fusion.4
  82.8 11.4 %while.18 = (s32[]{:T(128)}, f32[8,256]{1,0:T(8,128)S(1)}, f32[8,256]{1,0:T(8,128)S(1)}, f32[256,8,192]{0,2,1:T(8,128)}, bf16[1024,128]{0,1:T(8,128)(2,1)}, /*in...) while((s32[]{:T(128)}, f32[8,256]{1,0:T(8,128)S(1)}, ...), condition=%wide.region_5.0_spmd.clone, body=%wide.region_2.0_spmd.clone.sunk | while | flops 680669184 | bytes 29294832 | solution.py:74
  82.8 1.9 bitcast_reduce_fusion.2
  84.7 0.7 fusion.69
  86.1 1.3 bitcast_add_fusion.2
  87.4 1.1 copy-done.2
  88.5 1.9 bitcast_reduce_fusion.2
  91.8 1.3 bitcast_add_fusion.2
  93.1 1.1 copy-done.2
  94.2 1.5 divide_convert_fusion
  95.8 0.9 copy-done.3
  96.6 6.2 %convolution_bitcast_fusion = f32[1536,1536]{0,1:T(8,128)} fusion(bf16[256,1536]{0,1:T(8,128)(2,1)S(1)} %bitcast.77, bf16[1,256,1536]{2,1,0:T(8,128)(2,1)} %param.19), kind=kOutput, calls=%fused_computation.23 | convolution fusion | flops 1207959552 | bytes 11010048 | tf_op jit(solution)/shard_map/dot_general | solution.py:148
  102.8 5.1 %fusion.30 = bf16[1,256,1536]{2,1,0:T(8,128)(2,1)} fusion(bf16[256,1536]{0,1:T(8,128)(2,1)} %bitcast.78, bf16[1536,1536]{1,0:T(8,128)(2,1)} %param.18, bf16[256,1536]{1,0:T(8,128)(2,1)} %reduce_max.22), kind=kOutput, calls=%fused_computation.39 | convolution fusion | flops 1209925632 | bytes 7077888 | tf_op jit(solution)/shard_map/dot_general | solution.py:138
  107.9 178.3 %all-reduce.2.cloned.1.call-done = f32[1536,1536]{0,1:T(8,128)} async-done(((f32[1536,1536]{0,1:T(8,128)}), f32[1536,1536]{0,1:T(8,128)}) %all-reduce.2.cloned.1.call-update) | async-done | bytes 9437200 | tf_op jit(solution)/shard_map/psum | solution.py:151
  286.2 3.2 %constant_dynamic-slice_fusion = f32[384,1536]{0,1:T(8,128)} fusion(f32[1536,1536]{0,1:T(8,128)} %all-reduce.2.cloned.1.call-done, s32[]{:T(128)S(6)} %select_n.12), kind=kLoop, calls=%fused_computation.73 | loop fusion | bytes 4718596 | tf_op jit(solution)/shard_map/dynamic_slice | solution.py:152
  289.4 3.0 %copy.17 = f32[384,1536]{1,0:T(8,128)} copy(f32[384,1536]{0,1:T(8,128)} %constant_dynamic-slice_fusion) | data formatting | bytes 4718592
  (43 shorter events, 3.9 us)
Async XLA Ops:
  7.2 71.0 %copy-start = (bf16[1536,1024]{1,0:T(8,128)(2,1)S(1)}, bf16[1536,1024]{1,0:T(8,128)(2,1)}, u32[]{:S(2)}) copy-start(bf16[1536,1024]{1,0:T(8,128)(2,1)} %param.15) | copy-start | bytes 9437188
  7.2 279.1 %all-reduce.2.cloned.1.call-start = ((), (), s32[]{:S(2)}) async-start(), calls=%async_computation | async-start | bytes 18874368 | tf_op jit(solution)/shard_map/psum | solution.py:151
  8.1 16.3 %collective-permute-start.1 = (bf16[2,768]{1,0:T(2,128)(2,1)S(1)}, bf16[2,768]{1,0:T(2,128)(2,1)S(1)}, u32[]{:S(2)}, u32[]{:S(2)}) collective-permute-start(bf16[2,768]{1,0:T(2,128)(2,1)S(1)} %get-tuple-element.184), channel_id=1, source_target_pairs={{4,0},{8,4},{12,8},{5,1},{9,5},{13,9},{6,2},{10,6},{14,10},{7,3},{... | collective-permute-start | bytes 9224 | tf_op jit(solution)/shard_map/ppermute | solution.py:28
  9.5 10.6 %collective-permute-start = (bf16[2,768]{1,0:T(2,128)(2,1)S(1)}, bf16[2,768]{1,0:T(2,128)(2,1)S(1)}, u32[]{:S(2)}, u32[]{:S(2)}) collective-permute-start(bf16[2,768]{1,0:T(2,128)(2,1)S(1)} %get-tuple-element.185), channel_id=1, source_target_pairs={{0,4},{4,8},{8,12},{1,5},{5,9},{9,13},{2,6},{6,10},{10,14},{3,7},{... | collective-permute-start | bytes 9224 | tf_op jit(solution)/shard_map/ppermute | solution.py:26
  15.1 5.0 %copy-start.8 = (f32[1536]{0:T(1024)S(1)}, f32[1536]{0:T(1024)}, u32[]{:S(2)}) copy-start(f32[1536]{0:T(1024)} %param.13) | copy-start | bytes 18436
  20.1 4.3 %copy-start.7 = (bf16[1,512,768]{2,1,0:T(8,128)(2,1)S(1)}, bf16[1,512,768]{2,1,0:T(8,128)(2,1)}, u32[]{:S(2)}) copy-start(bf16[1,512,768]{2,1,0:T(8,128)(2,1)} %param.11) | copy-start | bytes 2359300
  29.3 12.0 %copy-start.9 = (f32[1536]{0:T(1024)S(1)}, f32[1536]{0:T(1024)}, u32[]{:S(2)}) copy-start(f32[1536]{0:T(1024)} %param.14) | copy-start | bytes 18436
  41.3 6.0 %copy-start.6 = (f32[256]{0:T(256)}, f32[256]{0:T(256)S(1)}, u32[]{:S(2)}) copy-start(f32[256]{0:T(256)S(1)} %add_rsqrt_fusion) | copy-start | bytes 3076
  80.3 0.9 copy-start.4
  80.3 1.0 copy-start.5
  84.6 1.4 copy-start.1
  87.3 1.1 copy-start.2
  90.4 1.4 copy-start.1
  93.1 1.1 copy-start.2
  95.7 0.9 copy-start.3
Sparse Core Ops, SparseCore 0:
  102.9 183.2 all-reduce.1
where the time goes:
time: 300 us; the launch traced here: 299 us
  waiting for transfers between devices  178 us (59%)
  matrix products  37.9 us (13%)
  blocking collectives  30.8 us (10%)
  local copies, waits for them, and re-layouts  18.6 us (6%)
  between operations  14.2 us (5%)
  other arithmetic  12.3 us (4%)
  starting transfers between devices  7.01 us (2%)
    psum x1, waiting for transfers between devices, local(): summed = lax.psum(whole_grad, ('seq', 'dp'))  178 us
    all_gather x1, blocking collectives, local(): lax.all_gather(key_rows, ('seq', 'head'), axis=0, tiled=True)  15.7 us
    all_gather x1, blocking collectives, local(): lax.all_gather(value_rows, ('seq', 'head'), axis=0, tiled=True)  15.1 us
    dot_general x3, matrix products, local(): jnp.dot(padded_rows[kernel_tap_index * DILATION_STEP:kernel_tap_index * D...  14.1 us
    dot_general x1, matrix products, local(): lax.dot_general(upstream, attended, (((0,), (0,)), ((), ())), preferred_e...  6.18 us
    reduce_max x1, other arithmetic, local(): jnp.max(activated.reshape(padded_row_count // 2, 2, -1), axis=1)  6.11 us
  transfers between devices with their start and end apart: 3, of which 1 were waited for; matrix products, arithmetic and copies ran while one was open for 5% of the time, Pallas kernels for 0%

commit v1 on v0

--- a/solution.py
+++ b/solution.py
@@ -1,8 +1,11 @@
+import functools
 import math
 
 import jax
 import jax.numpy as jnp
 from jax import lax
+from jax.experimental import pallas as pl
+from jax.experimental.pallas import tpu as pltpu
 from jax.sharding import PartitionSpec as P
 
 KEY = 128
@@ -72,6 +75,280 @@
         return (new_max, running_sum, weighted)
 
     return lax.fori_loop(0, total_keys // block_size, one_block, state_in)
+
+
+def signal_to(sem, where):
+    pl.semaphore_signal(sem, inc=1, device_id=where, device_id_type=pl.DeviceIdType.MESH)
+
+
+def remote(src, dst, send_sem, recv_sem, where):
+    return pltpu.make_async_remote_copy(
+        src_ref=src,
+        dst_ref=dst,
+        send_sem=send_sem,
+        recv_sem=recv_sem,
+        device_id=where,
+        device_id_type=pl.DeviceIdType.MESH,
+    )
+
+
+class Plan:
+    def __init__(self, tokens, width, columns, dp, seq):
+        self.tokens, self.width, self.columns = tokens, width, columns
+        self.dp, self.seq = dp, seq
+        self.levels = dp.bit_length() - 1
+        self.block = width // dp
+        self.rows = 128 if self.block % 128 == 0 else self.block
+        self.pieces = self.block // self.rows
+        self.chunk = 2 * VAL
+        self.chunks = columns // self.chunk
+        self.units = self.chunks * self.pieces
+
+    def scratch(self):
+        tile = (self.rows, self.chunk)
+        shapes = [
+            pltpu.VMEM((self.width, self.tokens), jnp.bfloat16),
+            pltpu.VMEM((self.chunks, self.tokens, self.chunk), jnp.bfloat16),
+            pltpu.VMEM((self.units,) + tile, jnp.float32),
+        ]
+        sends = self.levels + 2
+        for level in range(self.levels):
+            held = self.dp >> (level + 1)
+            shapes += [pltpu.VMEM((self.units, held) + tile, jnp.bfloat16)] * 2
+        shapes += [pltpu.VMEM((self.units,) + tile, jnp.bfloat16)] * 4
+        shapes += [pltpu.SemaphoreType.DMA((self.units,))] * (2 * sends)
+        return shapes
+
+
+def gradient_loop(plan, refs, out_ref):
+    cot_t, att, own = refs[:3]
+    levels, units = plan.levels, plan.units
+    pairs = refs[3 : 3 + 2 * levels]
+    ahead_out, ahead_in, back_out, back_in = refs[3 + 2 * levels : 7 + 2 * levels]
+    sems = refs[7 + 2 * levels :]
+    d = lax.axis_index("dp")
+    s = lax.axis_index("seq")
+    gap = 2
+    last = plan.seq - 1
+
+    def product(unit, p):
+        start = pl.multiple_of(
+            p * plan.block + (unit % plan.pieces) * plan.rows, plan.rows
+        )
+        return jnp.dot(
+            cot_t[pl.ds(start, plan.rows), :],
+            att[unit // plan.pieces],
+            preferred_element_type=jnp.float32,
+        )
+
+    def summed(unit, p, level):
+        value = product(unit, p)
+        for done in range(level):
+            value = value + pairs[2 * done + 1][unit, p // (2 << done)].astype(jnp.float32)
+        return value
+
+    def level_copy(unit, level):
+        step = 1 << level
+        peer = d + (1 - 2 * ((d // step) % 2)) * step
+        return remote(
+            pairs[2 * level].at[unit],
+            pairs[2 * level + 1].at[unit],
+            sems[2 * level].at[unit],
+            sems[2 * level + 1].at[unit],
+            {"dp": peer},
+        )
+
+    def ahead_copy(unit):
+        at = 2 * levels
+        return remote(
+            ahead_out.at[unit], ahead_in.at[unit], sems[at].at[unit], sems[at + 1].at[unit],
+            {"seq": s + 1},
+        )
+
+    def back_copy(unit):
+        at = 2 * levels + 2
+        return remote(
+            back_out.at[unit], back_in.at[unit], sems[at].at[unit], sems[at + 1].at[unit],
+            {"seq": s - 1},
+        )
+
+    def within(unit):
+        return jnp.logical_and(unit >= 0, unit < units)
+
+    def step_at(t, carry):
+        for level in range(levels):
+            unit = t - gap * level
+
+            @pl.when(within(unit))
+            def _(unit=unit, level=level):
+                if level > 0:
+                    level_copy(unit, level - 1).wait_recv()
+                step = 1 << level
+                base = d % step + (1 - (d // step) % 2) * step
+                for i in range(plan.dp >> (level + 1)):
+                    pairs[2 * level][unit, i] = summed(unit, base + i * 2 * step, level).astype(
+                        jnp.bfloat16
+                    )
+                level_copy(unit, level).start()
+
+        unit = t - gap * levels
+
+        @pl.when(within(unit))
+        def _():
+            if levels > 0:
+                level_copy(unit, levels - 1).wait_recv()
+            own[unit] = summed(unit, d, levels)
+
+        if last > 0:
+            fore = t - gap * (levels + s)
+
+            @pl.when(jnp.logical_and(within(fore), s == 0))
+            def _():
+                ahead_out[fore] = own[fore].astype(jnp.bfloat16)
+                ahead_copy(fore).start()
+
+            @pl.when(jnp.logical_and(within(fore), s > 0))
+            def _():
+                ahead_copy(fore).wait_recv()
+
+                @pl.when(s < last)
+                def _():
+                    ahead_out[fore] = (own[fore] + ahead_in[fore].astype(jnp.float32)).astype(
+                        jnp.bfloat16
+                    )
+                    ahead_copy(fore).start()
+
+            rear = t - gap * (levels + last - s)
+
+            @pl.when(jnp.logical_and(within(rear), s == last))
+            def _():
+                back_out[rear] = own[rear].astype(jnp.bfloat16)
+                back_copy(rear).start()
+
+            @pl.when(jnp.logical_and(within(rear), s < last))
+            def _():
+                back_copy(rear).wait_recv()
+
+                @pl.when(s > 0)
+                def _():
+                    back_out[rear] = (own[rear] + back_in[rear].astype(jnp.float32)).astype(
+                        jnp.bfloat16
+                    )
+                    back_copy(rear).start()
+
+        ready = t - gap * (levels + last)
+
+        def store(value):
+            row = pl.multiple_of((ready % plan.pieces) * plan.rows, plan.rows)
+            column = pl.multiple_of((ready // plan.pieces) * plan.chunk, plan.chunk)
+            out_ref[pl.ds(row, plan.rows), pl.ds(column, plan.chunk)] = value
+
+        if last == 0:
+
+            @pl.when(within(ready))
+            def _():
+                store(own[ready])
+
+        else:
+
+            @pl.when(jnp.logical_and(within(ready), s == 0))
+            def _():
+                store(own[ready] + back_in[ready].astype(jnp.float32))
+
+            @pl.when(jnp.logical_and(within(ready), s == last))
+            def _():
+                store(own[ready] + ahead_in[ready].astype(jnp.float32))
+
+            if last > 1:
+
+                @pl.when(
+                    jnp.logical_and(within(ready), jnp.logical_and(s > 0, s < last))
+                )
+                def _():
+                    store(
+                        own[ready]
+                        + ahead_in[ready].astype(jnp.float32)
+                        + back_in[ready].astype(jnp.float32)
+                    )
+
+        return carry
+
+    lax.fori_loop(0, units + gap * (levels + last), step_at, 0)
+
+    def drain(unit, carry):
+        for level in range(levels):
+            level_copy(unit, level).wait_send()
+        if last > 0:
+
+            @pl.when(s < last)
+            def _():
+                ahead_copy(unit).wait_send()
+
+            @pl.when(s > 0)
+            def _():
+                back_copy(unit).wait_send()
+
+        return carry
+
+    lax.fori_loop(0, units, drain, 0)
+
+
+def greet(plan):
+    barrier = pltpu.get_barrier_semaphore()
+    d = lax.axis_index("dp")
+    s = lax.axis_index("seq")
+    for level in range(plan.levels):
+        step = 1 << level
+        signal_to(barrier, {"dp": d + (1 - 2 * ((d // step) % 2)) * step})
+    if plan.seq > 1:
+
+        @pl.when(s > 0)
+        def _():
+            signal_to(barrier, {"seq": s - 1})
+
+        @pl.when(s < plan.seq - 1)
+        def _():
+            signal_to(barrier, {"seq": s + 1})
+
+    if plan.seq == 1:
+        pl.semaphore_wait(barrier, plan.levels)
+        return
+    edge = jnp.logical_or(s == 0, s == plan.seq - 1)
+
+    @pl.when(edge)
+    def _():
+        pl.semaphore_wait(barrier, plan.levels + 1)
+
+    @pl.when(jnp.logical_not(edge))
+    def _():
+        pl.semaphore_wait(barrier, plan.levels + 2)
+
+
+def gradient_kernel(plan, cot_ref, att_ref, out_ref, *refs):
+    greet(plan)
+    refs[0][...] = jnp.transpose(cot_ref[...])
+    for c in range(plan.chunks):
+        refs[1][c] = att_ref[:, c * plan.chunk : (c + 1) * plan.chunk]
+    gradient_loop(plan, refs, out_ref)
+
+
+def reduced_gradient(upstream, attended):
+    plan = Plan(
+        upstream.shape[0], upstream.shape[1], attended.shape[1],
+        lax.axis_size("dp"), lax.axis_size("seq"),
+    )
+    whole = pl.BlockSpec(memory_space=pltpu.VMEM)
+    return pl.pallas_call(
+        functools.partial(gradient_kernel, plan),
+        out_shape=jax.ShapeDtypeStruct((plan.block, plan.columns), jnp.float32),
+        in_specs=[whole, whole],
+        out_specs=whole,
+        scratch_shapes=plan.scratch(),
+        compiler_params=pltpu.CompilerParams(
+            collective_id=0, has_side_effects=True, vmem_limit_bytes=56 * 2**20
+        ),
+        name="reduced_gradient",
+    )(upstream, attended)
 
 
 def local(x_in, kernel_weight, conv_bias, norm_gain, w_query, w_key, w_value, w_out, cotangent):
@@ -122,10 +399,13 @@
         jnp.zeros((local_heads, token_count), jnp.float32),
         jnp.zeros((token_count, local_heads, VAL), jnp.float32),
     )
+    both = lax.all_gather(
+        jnp.concatenate([key_rows, value_rows], axis=1), ("seq", "head"), axis=0, tiled=True
+    )
     final_state = attend_pieces(
         queries,
-        lax.all_gather(key_rows, ("seq", "head"), axis=0, tiled=True),
-        lax.all_gather(value_rows, ("seq", "head"), axis=0, tiled=True),
+        both[:, :KEY],
+        both[:, KEY:],
         start_state,
     )
     running_max, running_sum, weighted = final_state
@@ -144,12 +424,7 @@
     ).astype(jnp.float32)
     mixed = (pooled.astype(jnp.float32) + jnp.transpose(projected)).astype(jnp.bfloat16)[None]
     upstream = cotangent[0]
-    dp_rows = upstream.shape[1] // lax.axis_size("dp")
-    whole_grad = lax.dot_general(
-        upstream, attended, (((0,), (0,)), ((), ())), preferred_element_type=jnp.float32
-    )
-    summed = lax.psum(whole_grad, ("seq", "dp"))
-    gradient = lax.dynamic_slice_in_dim(summed, lax.axis_index("dp") * dp_rows, dp_rows, 0)
+    gradient = reduced_gradient(upstream, attended)
     return (mixed, gradient)
 
 

time: 300 us -> 144 us (0.48)
  waiting for transfers between devices: 178 us -> 0.01 us
  Pallas kernels: 0 us -> 48.3 us
  between operations: 14.2 us -> 0.86 us
  blocking collectives: 30.8 us -> 19 us
  local copies, waits for them, and re-layouts: 18.6 us -> 14.3 us
  matrix products: 37.9 us -> 41.7 us
    psum x1 -> x0, waiting for transfers between devices: 178 us -> none  [local(): summed = lax.psum(whole_grad, ('seq', 'dp'))]
    pallas_call x0 -> x1, Pallas kernels: none -> 48.3 us  [reduced_gradient(): pl.pallas_call(functools.partial(gradient_kernel, plan), out_shape=jax.Sh...]
    all_gather x2 -> x1, blocking collectives: 30.8 us -> 19 us  [local(): lax.all_gather(jnp.concatenate([key_rows, value_rows], axis=1), ('seq', '...]
    dot_general x2, matrix products: 2.55 us -> 9.53 us  [one_block(): jnp.einsum('htu,uv->thv', weights.astype(jnp.bfloat16), value_block, pref...]
    dot_general x1 -> x0, matrix products: 6.18 us -> none  [local(): lax.dot_general(upstream, attended, (((0,), (0,)), ((), ())), preferred_e...]
    dot_general x2, matrix products: 3.71 us -> 7.6 us  [one_block(): jnp.einsum('thd,ud->htu', queries, key_block, preferred_element_type=jnp....]
    dynamic_slice x1 -> x0, local copies, waits for them, and re-layouts: 3.21 us -> none  [local(): lax.dynamic_slice_in_dim(summed, lax.axis_index('dp') * dp_rows, dp_rows, 0)]
  transfers between devices with their start and end apart: 3 -> 2, of which waited for: 1 -> 0; matrix products, arithmetic and copies ran while one was open for 5% -> 6% of each run, Pallas kernels for 0% -> 0%
where the time goes in v1:
time: 144 us
  Pallas kernels  48.3 us (34%)
  matrix products  41.7 us (29%)
  blocking collectives  19 us (13%)
  local copies, waits for them, and re-layouts  14.3 us (10%)
  other arithmetic  13.2 us (9%)
  starting transfers between devices  6.35 us (4%)
    pallas_call x1, Pallas kernels, reduced_gradient(): pl.pallas_call(functools.partial(gradient_kernel, plan), out_shape=jax.Sh...  48.3 us
    all_gather x1, blocking collectives, local(): lax.all_gather(jnp.concatenate([key_rows, value_rows], axis=1), ('seq', '...  19 us
    dot_general x3, matrix products, local(): jnp.dot(padded_rows[kernel_tap_index * DILATION_STEP:kernel_tap_index * D...  14.1 us
    dot_general x2, matrix products, one_block(): jnp.einsum('htu,uv->thv', weights.astype(jnp.bfloat16), value_block, pref...  9.53 us
    dot_general x2, matrix products, one_block(): jnp.einsum('thd,ud->htu', queries, key_block, preferred_element_type=jnp....  7.6 us
    reduce_max x1, other arithmetic, local(): jnp.max(activated.reshape(padded_row_count // 2, 2, -1), axis=1)  6.11 us
    ppermute x1, starting transfers between devices, padded(): lax.ppermute(tail, axis, [(i, (i + 1) % count) for i in range(ends)])  5.05 us
    dot_general x1, matrix products, local(): lax.dot_general(w_out, attended, (((0,), (1,)), ((), ())), preferred_elem...  4.77 us
  transfers between devices with their start and end apart: 2, of which 0 were waited for; matrix products, arithmetic and copies ran while one was open for 6% of the time, Pallas kernels for 0%

profile of v1, /device:TPU:0, one launch (start us, length us, event | category | flops | bytes accessed | tf_op | source)
XLA Modules:
  0.0 143.7 jit_solution(4584771153966449722)
XLA Ops:
  0.6 0.9 slice_bitcast_fusion
  1.5 5.1 %collective-permute-start = (bf16[2,768]{1,0:T(2,128)(2,1)S(1)}, bf16[2,768]{1,0:T(2,128)(2,1)S(1)}, u32[]{:S(2)}, u32[]{:S(2)}) collective-permute-start(bf16[2,768]{1,0:T(2,128)(2,1)S(1)} %get-tuple-element.190), channel_id=1, source_target_pairs={{0,4},{4,8},{8,12},{1,5},{5,9},{9,13},{2,6},{6,10},{10,14},{3,7},{... | collective-permute-start | bytes 9224 | tf_op jit(solution)/shard_map/ppermute | solution.py:29
  6.6 1.3 collective-permute-start.1
  7.9 4.9 %fusion.32 = f32[512,1536]{1,0:T(8,128)} fusion(bf16[3,768,1536]{2,1,0:T(8,128)(2,1)} %param.12, bf16[1,512,768]{2,1,0:T(8,128)(2,1)} %param.11), kind=kOutput, calls=%fused_computation.42 | convolution fusion | flops 1207959552 | bytes 6291456 | tf_op jit(solution)/shard_map/dot_general | solution.py:363
  12.9 4.3 %fusion.19 = f32[512,1536]{1,0:T(8,128)S(1)} fusion(f32[512,1536]{1,0:T(8,128)} %fusion.32, bf16[3,768,1536]{2,1,0:T(8,128)(2,1)} %param.12, f32[1536]{0:T(1024)S(1)} %copy-done.11, bf16[512,768]{1,0:T(8,128)(2,1)} %bitcast.76, bf16[2,768]{1,0:T(2,128)(2,1)S(1)} %collective-permute-done), kind=kOutput, calls=%fused_computation.26 | convolution fusion | flops 1211105280 | bytes 9446400 | tf_op jit(solution)/shard_map/dot_general | solution.py:363
  17.2 4.9 %fusion.26 = bf16[512,1536]{1,0:T(8,128)(2,1)} fusion(f32[512,1536]{1,0:T(8,128)S(1)} %fusion.19, bf16[3,768,1536]{2,1,0:T(8,128)(2,1)} %param.12, bf16[2,768]{1,0:T(2,128)(2,1)S(1)} %collective-permute-done.1, bf16[512,768]{1,0:T(8,128)(2,1)S(1)} %bitcast.77), kind=kOutput, calls=%fused_computation.33 | convolution fusion | flops 1217396736 | bytes 7867392 | tf_op jit(solution)/shard_map/dot_general | solution.py:363
  22.1 4.5 %reshape.92 = bf16[256,2,1536]{2,1,0:T(2,128)(2,1)} reshape(bf16[512,1536]{1,0:T(8,128)(2,1)} %fusion.26) | data formatting | bytes 3145728 | tf_op jit(solution)/shard_map/reshape | solution.py:372
  26.6 6.1 %reduce_max.22 = bf16[256,1536]{1,0:T(8,128)(2,1)} reduce(bf16[256,2,1536]{2,1,0:T(2,128)(2,1)} %reshape.92, bf16[]{:T(256)} %constant.143), dimensions={1}, to_apply=%region_0.0 | reduce | flops 393216 | bytes 2359298 | tf_op jit(solution)/shard_map/reduce_max | solution.py:372
  32.7 1.4 fusion.38
  34.1 1.7 %fusion.49 = f32[256,128]{0,1:T(8,128)S(1)} fusion(bf16[1536,128]{1,0:T(8,128)(2,1)} %param.16, f32[1536]{0:T(1024)S(1)} %copy-done.12, f32[256]{0:T(256)S(1)} %add_rsqrt_fusion, bf16[256,1536]{1,0:T(8,128)(2,1)} %reduce_max.22), kind=kOutput, calls=%fused_computation.75 | convolution fusion | flops 102236160 | bytes 1317888 | tf_op jit(solution)/shard_map/dot_general | solution.py:392
  35.8 1.8 %convolution_convert_fusion.1 = bf16[256,192]{0,1:T(8,128)(2,1)S(1)} fusion(bf16[1536,192]{0,1:T(8,128)(2,1)} %param.17, f32[1536]{0:T(1024)S(1)} %copy-done.12, f32[256]{0:T(256)S(1)} %add_rsqrt_fusion, bf16[256,1536]{1,0:T(8,128)(2,1)} %reduce_max.22), kind=kOutput, calls=%fused_computation.53 | convolution fusion | flops 152616960 | bytes 1481728 | tf_op jit(solution)/shard_map/dot_general | solution.py:394
  38.0 19.0 %all_gather.4 = bf16[1024,320]{0,1:T(8,128)(2,1)S(1)} all-gather(bf16[256,320]{0,1:T(8,128)(2,1)S(1)} %pad_maximum_fusion.5), channel_id=1, replica_groups=mesh['groups'=2,'seq'=4,'dp'=4,'head'=1] {'seq','head'}, dimensions={0}, use_global_device_ids=true | all-gather | bytes 819200 | tf_op jit(solution)/shard_map/all_gather | solution.py:402
  57.0 0.8 copy-done.3
  57.8 0.7 slice.64
  58.5 0.8 copy.20
  59.3 0.7 copy.22
  60.0 2.2 %convolution_bitcast_fusion = f32[32,8,8,128]{3,1,2,0:T(8,128)S(1)} fusion(bf16[1536,1024]{1,0:T(8,128)(2,1)S(1)} %copy-done, f32[1536]{0:T(1024)S(1)} %copy-done.12, f32[256]{0:T(256)S(1)} %add_rsqrt_fusion, bf16[256,1536]{1,0:T(8,128)(2,1)} %reduce_max.22), kind=kOutput, calls=%fused_computation.52 | convolution fusion | flops 806879232 | bytes 4987904 | tf_op jit(solution)/shard_map/dot_general | solution.py:382
  63.6 1.1 pad_maximum_fusion.4
  64.7 19.8 %while.18 = (s32[]{:T(128)}, f32[8,256]{1,0:T(8,128)S(1)}, f32[8,256]{1,0:T(8,128)}, f32[256,8,192]{0,2,1:T(8,128)}, bf16[1024,128]{0,1:T(8,128)(2,1)}, /*index=...) while((s32[]{:T(128)}, f32[8,256]{1,0:T(8,128)S(1)}, ...), condition=%wide.region_5.0_spmd.clone, body=%wide.region_2.0_spmd.clone.sunk | while | flops 680669184 | bytes 33554688 | solution.py:77
  64.7 3.8 %bitcast_reduce_fusion.2 = (f32[8,256]{1,0:T(8,128)S(1)}, f32[512,256,8]{1,0,2:T(8,128)}) fusion(bf16[256,8,128]{2,0,1:T(8,128)(2,1)} %get-tuple-element.275, bf16[1024,128]{0,1:T(8,128)(2,1)} %get-tuple-element.274, s32[]{:T(128)S(6)} %select_n.11), kind=kOutput, calls=%fused_computation.1.clone.1 | convolution fusion | flops 270530560 | bytes 4857860 | tf_op jit(solution)/shard_map/while/body/eval_jaxpr/thd,ud->htu/dot_general | solution.py:62
  68.5 4.5 %bitcast_add_fusion.2 = f32[256,8,192]{0,2,1:T(8,128)} fusion(f32[256,8,192]{0,2,1:T(8,128)} %get-tuple-element.262, f32[512,256,8]{1,0,2:T(8,128)} %get-tuple-element.246, f32[8,256]{1,0:T(8,128)S(1)} %get-tuple-element.271, f32[256,8]{0,1:T(8,128)S(1)} %get-tuple-element.247, pred[]{:T(512)S(6)} %compare.3, ...), kind=kOutput, calls=%fused_computation.8.clone.1 | convolution fusion | flops 406978560 | bytes 7553029 | tf_op jit(solution)/shard_map/while/body/eval_jaxpr/htu,uv->thv/dot_general | solution.py:69
  73.0 0.7 fusion.67
  73.8 0.6 copy-done.9
  74.4 3.8 %bitcast_reduce_fusion.2 = (f32[8,256]{1,0:T(8,128)S(1)}, f32[512,256,8]{1,0,2:T(8,128)}) fusion(bf16[256,8,128]{2,0,1:T(8,128)(2,1)} %get-tuple-element.275, bf16[1024,128]{0,1:T(8,128)(2,1)} %get-tuple-element.274, s32[]{:T(128)S(6)} %select_n.11), kind=kOutput, calls=%fused_computation.1.clone.1 | convolution fusion | flops 270530560 | bytes 4857860 | tf_op jit(solution)/shard_map/while/body/eval_jaxpr/thd,ud->htu/dot_general | solution.py:62
  78.2 5.0 %bitcast_add_fusion.2 = f32[256,8,192]{0,2,1:T(8,128)} fusion(f32[256,8,192]{0,2,1:T(8,128)} %get-tuple-element.262, f32[512,256,8]{1,0,2:T(8,128)} %get-tuple-element.246, f32[8,256]{1,0:T(8,128)S(1)} %get-tuple-element.271, f32[256,8]{0,1:T(8,128)S(1)} %get-tuple-element.247, pred[]{:T(512)S(6)} %compare.3, ...), kind=kOutput, calls=%fused_computation.8.clone.1 | convolution fusion | flops 406978560 | bytes 7553029 | tf_op jit(solution)/shard_map/while/body/eval_jaxpr/htu,uv->thv/dot_general | solution.py:69
  83.2 0.7 fusion.67
  83.9 0.6 copy-done.9
  84.5 2.4 %divide_convert_fusion = bf16[256,8,192]{0,2,1:T(8,128)(2,1)} fusion(f32[256,8,192]{0,2,1:T(8,128)} %get-tuple-element.127, f32[256,8]{0,1:T(8,128)} %bitcast.75), kind=kLoop, calls=%fused_computation.51 | loop fusion | flops 786432 | bytes 2367488 | tf_op jit(solution)/shard_map/convert_element_type | solution.py:414
  86.9 2.3 %copy.24.att_ref = bf16[256,1536]{1,0:T(8,128)(2,1)} copy(bf16[256,1536]{0,1:T(8,128)(2,1)} %bitcast.72) | data formatting | bytes 1572864 | tf_op jit(solution)/shard_map/reshape | solution.py:415
  89.2 48.3 %reduced_gradient.1 = f32[384,1536]{1,0:T(8,128)} custom-call(bf16[256,1536]{1,0:T(8,128)(2,1)} %bitcast.74, bf16[256,1536]{1,0:T(8,128)(2,1)} %copy.24.att_ref), custom_call_target="tpu_custom_call" | custom-call | tf_op jit(solution)/shard_map/reduced_gradient/pallas_call | solution.py:341
  137.5 4.8 %fusion.30 = bf16[1,256,1536]{2,1,0:T(8,128)(2,1)} fusion(bf16[256,1536]{0,1:T(8,128)(2,1)S(1)} %bitcast.73, bf16[1536,1536]{1,0:T(8,128)(2,1)} %param.18, bf16[256,1536]{1,0:T(8,128)(2,1)S(1)} %copy-done.4), kind=kOutput, calls=%fused_computation.38 | convolution fusion | flops 1209925632 | bytes 7077888 | tf_op jit(solution)/shard_map/dot_general | solution.py:418
  142.3 1.4 copy.47
  (50 shorter events, 1.8 us)
Async XLA Ops:
  0.6 59.4 %copy-start = (bf16[1536,1024]{1,0:T(8,128)(2,1)S(1)}, bf16[1536,1024]{1,0:T(8,128)(2,1)}, u32[]{:S(2)}) copy-start(bf16[1536,1024]{1,0:T(8,128)(2,1)} %param.15) | copy-start | bytes 9437188
  1.5 11.4 %collective-permute-start = (bf16[2,768]{1,0:T(2,128)(2,1)S(1)}, bf16[2,768]{1,0:T(2,128)(2,1)S(1)}, u32[]{:S(2)}, u32[]{:S(2)}) collective-permute-start(bf16[2,768]{1,0:T(2,128)(2,1)S(1)} %get-tuple-element.190), channel_id=1, source_target_pairs={{0,4},{4,8},{8,12},{1,5},{5,9},{9,13},{2,6},{6,10},{10,14},{3,7},{... | collective-permute-start | bytes 9224 | tf_op jit(solution)/shard_map/ppermute | solution.py:29
  6.6 10.6 %collective-permute-start.1 = (bf16[2,768]{1,0:T(2,128)(2,1)S(1)}, bf16[2,768]{1,0:T(2,128)(2,1)S(1)}, u32[]{:S(2)}, u32[]{:S(2)}) collective-permute-start(bf16[2,768]{1,0:T(2,128)(2,1)S(1)} %get-tuple-element.189), channel_id=1, source_target_pairs={{4,0},{8,4},{12,8},{5,1},{9,5},{13,9},{6,2},{10,6},{14,10},{7,3},{... | collective-permute-start | bytes 9224 | tf_op jit(solution)/shard_map/ppermute | solution.py:31
  7.9 5.0 %copy-start.11 = (f32[1536]{0:T(1024)S(1)}, f32[1536]{0:T(1024)}, u32[]{:S(2)}) copy-start(f32[1536]{0:T(1024)} %param.13) | copy-start | bytes 18436
  12.9 4.3 %copy-start.10 = (bf16[1,512,768]{2,1,0:T(8,128)(2,1)S(1)}, bf16[1,512,768]{2,1,0:T(8,128)(2,1)}, u32[]{:S(2)}) copy-start(bf16[1,512,768]{2,1,0:T(8,128)(2,1)} %param.11) | copy-start | bytes 2359300
  22.1 12.0 %copy-start.12 = (f32[1536]{0:T(1024)S(1)}, f32[1536]{0:T(1024)}, u32[]{:S(2)}) copy-start(f32[1536]{0:T(1024)} %param.14) | copy-start | bytes 18436
  57.0 0.8 copy-start.3
  62.2 0.9 copy-start.6
  62.2 1.0 copy-start.7
  62.8 1.9 %slice-start = ((bf16[1024,320]{0,1:T(8,128)(2,1)}), bf16[1024,192]{0,1:T(8,128)(2,1)S(1)}, s32[]{:S(2)}) async-start(bf16[1024,320]{0,1:T(8,128)(2,1)} %copy-done.3), calls=%async_computation | async-start | bytes 786432 | tf_op jit(solution)/shard_map/slice | solution.py:408
  68.5 4.5 %copy-start.1 = (f32[512,256,8]{1,0,2:T(8,128)S(1)}, f32[512,256,8]{1,0,2:T(8,128)}, u32[]{:S(2)}) copy-start(f32[512,256,8]{1,0,2:T(8,128)} %get-tuple-element.246) | copy-start | bytes 12582916 | tf_op jit(solution)/shard_map/while
  73.0 0.7 copy-start.8
  73.8 0.6 copy-start.9
  78.2 5.0 %copy-start.1 = (f32[512,256,8]{1,0,2:T(8,128)S(1)}, f32[512,256,8]{1,0,2:T(8,128)}, u32[]{:S(2)}) copy-start(f32[512,256,8]{1,0,2:T(8,128)} %get-tuple-element.246) | copy-start | bytes 12582916 | tf_op jit(solution)/shard_map/while
  83.2 0.7 copy-start.8
  83.9 0.6 copy-start.9
  89.2 48.3 %copy-start.4 = (bf16[256,1536]{1,0:T(8,128)(2,1)S(1)}, bf16[256,1536]{1,0:T(8,128)(2,1)}, u32[]{:S(2)}) copy-start(bf16[256,1536]{1,0:T(8,128)(2,1)} %reduce_max.22) | copy-start | bytes 2359300
  89.2 48.3 %copy-start.5 = (bf16[256,8,192]{0,2,1:T(8,128)(2,1)S(1)}, bf16[256,8,192]{0,2,1:T(8,128)(2,1)}, u32[]{:S(2)}) copy-start(bf16[256,8,192]{0,2,1:T(8,128)(2,1)} %divide_convert_fusion) | copy-start | bytes 2359300
  137.5 4.8 %copy-start.2 = (f32[384,1536]{1,0:T(8,128)S(1)}, f32[384,1536]{1,0:T(8,128)}, u32[]{:S(2)}) copy-start(f32[384,1536]{1,0:T(8,128)} %reduced_gradient.1) | copy-start | bytes 7077892

commit v2 on v1

--- a/solution.py
+++ b/solution.py
@@ -6,6 +6,7 @@
 from jax import lax
 from jax.experimental import pallas as pl
 from jax.experimental.pallas import tpu as pltpu
+import numpy as np
 from jax.sharding import PartitionSpec as P
 
 KEY = 128
@@ -120,7 +121,7 @@
         return shapes
 
 
-def gradient_loop(plan, refs, out_ref):
+def gradient_loop(plan, refs, out_ref, produce=None, least=0):
     cot_t, att, own = refs[:3]
     levels, units = plan.levels, plan.units
     pairs = refs[3 : 3 + 2 * levels]
@@ -176,6 +177,8 @@
         return jnp.logical_and(unit >= 0, unit < units)
 
     def step_at(t, carry):
+        if produce is not None:
+            produce(t)
         for level in range(levels):
             unit = t - gap * level
 
@@ -273,7 +276,7 @@
 
         return carry
 
-    lax.fori_loop(0, units + gap * (levels + last), step_at, 0)
+    lax.fori_loop(0, max(least, units + gap * (levels + last)), step_at, 0)
 
     def drain(unit, carry):
         for level in range(levels):
@@ -349,6 +352,314 @@
         ),
         name="reduced_gradient",
     )(upstream, attended)
+
+
+def meet(plan):
+    barrier = pltpu.get_barrier_semaphore()
+    d = lax.axis_index("dp")
+    s = lax.axis_index("seq")
+    for level in range(plan.levels):
+        step = 1 << level
+        signal_to(barrier, {"dp": d + (1 - 2 * ((d // step) % 2)) * step})
+    for j in range(1, plan.seq):
+        signal_to(barrier, {"seq": (s + j) % plan.seq})
+    pl.semaphore_wait(barrier, plan.levels + plan.seq - 1)
+
+
+EDGE = 16
+TILE = 256
+
+
+def section_kernel(plan, *refs):
+    (x_hbm, conv_hbm, bias, gain, query_hbm, key_hbm, value_hbm, out_hbm, cot_hbm, turn_hbm) = refs[:10]
+    mixed, grad_out = refs[10:12]
+    (
+        x_rows, conv_w, query_w, key_w, value_w, out_w, cot, turn, fetched,
+        edges, edge_sems, spread, stacked, pooled, normed, queries, keys, values, kv_sems,
+    ) = refs[12:31]
+    gradient_refs = refs[31:]
+    cot_t, att = gradient_refs[:2]
+    tokens, rows = plan.tokens, 2 * plan.tokens
+    s = lax.axis_index("seq")
+    last = plan.seq - 1
+    tiles = plan.width // TILE
+    taps, channels = KERNEL_TAPS, x_rows.shape[1]
+
+    def conv_fetch(n):
+        return pltpu.make_async_copy(
+            conv_hbm.at[:, pl.ds(pl.multiple_of(n * TILE, TILE), TILE)],
+            conv_w.at[n],
+            fetched.at[8 + n],
+        )
+
+    x_fetch = pltpu.make_async_copy(x_hbm, x_rows, fetched.at[0])
+    key_fetch = pltpu.make_async_copy(key_hbm, key_w, fetched.at[1])
+    value_fetch = pltpu.make_async_copy(value_hbm, value_w, fetched.at[2])
+    turn_fetch = pltpu.make_async_copy(
+        turn_hbm.at[pl.ds(pl.multiple_of(s * tokens, tokens), tokens)], turn, fetched.at[3]
+    )
+    query_fetch = pltpu.make_async_copy(query_hbm, query_w, fetched.at[4])
+    cot_fetch = pltpu.make_async_copy(cot_hbm, cot, fetched.at[5])
+    out_fetch = pltpu.make_async_copy(out_hbm, out_w, fetched.at[6])
+    x_fetch.start()
+    for n in range(tiles):
+        conv_fetch(n).start()
+    for fetch in (key_fetch, value_fetch, turn_fetch, query_fetch, cot_fetch, out_fetch):
+        fetch.start()
+
+    meet(plan)
+
+    def edge_ahead():
+        return remote(
+            x_hbm.at[pl.ds(rows - EDGE, EDGE)], edges.at[0], edge_sems.at[0], edge_sems.at[1],
+            {"seq": s + 1},
+        )
+
+    def edge_back():
+        return remote(
+            x_hbm.at[pl.ds(0, EDGE)], edges.at[1], edge_sems.at[2], edge_sems.at[3],
+            {"seq": s - 1},
+        )
+
+    blocks = channels // 128
+    if last > 0:
+
+        @pl.when(s < last)
+        def _():
+            edge_ahead().start()
+
+        @pl.when(s > 0)
+        def _():
+            edge_back().start()
+
+    x_fetch.wait()
+    for j in range(blocks):
+        spread[j, EDGE : EDGE + rows, :] = x_rows[:, j * 128 : (j + 1) * 128].astype(jnp.float32)
+    blank = jnp.zeros((EDGE, 128), jnp.float32)
+
+    def put_edge(which, start, there):
+        @pl.when(there)
+        def _():
+            if last > 0:
+                (edge_ahead if which == 0 else edge_back)().wait_recv()
+                for j in range(blocks):
+                    spread[j, start : start + EDGE, :] = edges[
+                        which, :, j * 128 : (j + 1) * 128
+                    ].astype(jnp.float32)
+
+        @pl.when(jnp.logical_not(there))
+        def _():
+            for j in range(blocks):
+                spread[j, start : start + EDGE, :] = blank
+
+    put_edge(0, 0, s > 0)
+    put_edge(1, EDGE + rows, s < last)
+    for parity in range(2):
+        for tap in range(taps):
+            for j in range(blocks):
+                start = EDGE + parity + DILATION_STEP * (tap - 1)
+                lane = tap * channels + j * 128
+                stacked[parity * tokens : (parity + 1) * tokens, lane : lane + 128] = spread[
+                    j, pl.ds(start, tokens, stride=2), :
+                ].astype(jnp.bfloat16)
+
+    def conv_tile(n, carry):
+        conv_fetch(n).wait()
+        columns = pl.ds(pl.multiple_of(n * TILE, TILE), TILE)
+        pre = (
+            jnp.dot(stacked[...], conv_w[n], preferred_element_type=jnp.float32)
+            + bias[:, columns]
+        )
+        inner = math.sqrt(2.0 / math.pi) * (pre + 0.044715 * (pre * pre * pre))
+        activated = pre * (0.5 * (1.0 + jnp.tanh(inner)))
+        pooled[:, columns] = jnp.maximum(activated[:tokens], activated[tokens:]).astype(
+            jnp.bfloat16
+        )
+        return carry
+
+    lax.fori_loop(0, tiles, conv_tile, 0)
+
+    part = 32
+
+    def norm_part(i, carry):
+        here = pl.ds(pl.multiple_of(i * part, part), part)
+        wide = pooled[here, :].astype(jnp.float32)
+        squares = jnp.mean(wide * wide, axis=-1, keepdims=True)
+        normed[here, :] = (wide * lax.rsqrt(squares + norm_eps) * gain[...]).astype(jnp.bfloat16)
+        return carry
+
+    lax.fori_loop(0, tokens // part, norm_part, 0)
+
+    key_fetch.wait()
+    value_fetch.wait()
+    turn_fetch.wait()
+
+    def turned(vectors):
+        return (
+            vectors * turn[:, :KEY] + pltpu.roll(vectors, KEY // 2, 1) * turn[:, KEY:]
+        ).astype(jnp.bfloat16)
+
+    keys[s] = turned(jnp.dot(normed[...], key_w[...], preferred_element_type=jnp.float32))
+    values[s] = jnp.dot(normed[...], value_w[...], preferred_element_type=jnp.float32).astype(
+        jnp.bfloat16
+    )
+
+    def kv_copies(owner, j, peer):
+        at = 4 * (j - 1)
+        return (
+            remote(keys.at[owner], keys.at[owner], kv_sems.at[at], kv_sems.at[at + 1], {"seq": peer}),
+            remote(
+                values.at[owner], values.at[owner], kv_sems.at[at + 2], kv_sems.at[at + 3],
+                {"seq": peer},
+            ),
+        )
+
+    for j in range(1, plan.seq):
+        for copy in kv_copies(s, j, (s + j) % plan.seq):
+            copy.start()
+
+    query_fetch.wait()
+
+    def query_pair(c, carry):
+        pair = jnp.dot(
+            normed[...],
+            query_w[:, pl.ds(pl.multiple_of(c * 2 * KEY, 2 * KEY), 2 * KEY)],
+            preferred_element_type=jnp.float32,
+        )
+        queries[2 * c] = turned(pair[:, :KEY])
+        queries[2 * c + 1] = turned(pair[:, KEY:])
+        return carry
+
+    lax.fori_loop(0, plan.chunks, query_pair, 0)
+    cot_fetch.wait()
+    cot_t[...] = jnp.transpose(cot[...])
+    out_fetch.wait()
+    for j in range(1, plan.seq):
+        owner = (s + plan.seq - j) % plan.seq
+        for copy in kv_copies(owner, j, (s + j) % plan.seq):
+            copy.wait_recv()
+
+    def attend_head(h):
+        scores = lax.dot_general(
+            queries[h],
+            keys[...].reshape(plan.seq * tokens, KEY),
+            (((1,), (1,)), ((), ())),
+            preferred_element_type=jnp.float32,
+        )
+        peak = jnp.max(scores, axis=-1, keepdims=True)
+        weights = jnp.exp2((scores - peak) * (KEY ** (-0.5) * math.log2(math.e)))
+        total = jnp.sum(weights, axis=-1, keepdims=True)
+        weighted = jnp.dot(
+            weights.astype(jnp.bfloat16),
+            values[...].reshape(plan.seq * tokens, VAL),
+            preferred_element_type=jnp.float32,
+        )
+        return weighted / total
+
+    def produce(t):
+        @pl.when(jnp.logical_and(t < plan.units, t % plan.pieces == 0))
+        def _():
+            c = t // plan.pieces
+            att[c] = jnp.concatenate([attend_head(2 * c), attend_head(2 * c + 1)], axis=1).astype(
+                jnp.bfloat16
+            )
+
+        @pl.when(jnp.logical_and(t >= plan.units, t < plan.units + tiles))
+        def _():
+            columns = pl.ds(pl.multiple_of((t - plan.units) * TILE, TILE), TILE)
+            total = pooled[:, columns].astype(jnp.float32)
+            for c in range(plan.chunks):
+                total = total + jnp.dot(
+                    att[c],
+                    out_w[c * plan.chunk : (c + 1) * plan.chunk, columns],
+                    preferred_element_type=jnp.float32,
+                )
+            mixed[:, columns] = total.astype(jnp.bfloat16)
+
+    gradient_loop(plan, gradient_refs, grad_out, produce, plan.units + tiles)
+
+    for j in range(1, plan.seq):
+        for copy in kv_copies(s, j, (s + j) % plan.seq):
+            copy.wait_send()
+    if last > 0:
+
+        @pl.when(s < last)
+        def _():
+            edge_ahead().wait_send()
+
+        @pl.when(s > 0)
+        def _():
+            edge_back().wait_send()
+
+
+def turn_table(count):
+    frequency = np.exp(
+        np.float32(-math.log(rope_base) * 2.0) * np.arange(KEY // 2, dtype=np.float32) / KEY
+    ).astype(np.float32)
+    angles = np.arange(count, dtype=np.float32)[:, None] * frequency[None, :]
+    cosine, sines = np.cos(angles), np.sin(angles)
+    return np.concatenate([cosine, cosine, -sines, sines], axis=1).astype(np.float32)
+
+
+def section(x_in, kernel_weight, conv_bias, norm_gain, w_query, w_key, w_value, w_out, cotangent):
+    inputs, upstream = x_in[0], cotangent[0]
+    rows, channels = inputs.shape
+    width = kernel_weight.shape[2]
+    plan = Plan(
+        rows // 2, width, w_out.shape[0], lax.axis_size("dp"), lax.axis_size("seq")
+    )
+    tokens, seq, tiles = plan.tokens, plan.seq, width // TILE
+    depth = KERNEL_TAPS * channels
+    bf = jnp.bfloat16
+    held = pl.BlockSpec(memory_space=pltpu.VMEM)
+    away = pl.BlockSpec(memory_space=pl.ANY)
+    mixed, gradient = pl.pallas_call(
+        functools.partial(section_kernel, plan),
+        out_shape=(
+            jax.ShapeDtypeStruct((tokens, width), bf),
+            jax.ShapeDtypeStruct((plan.block, plan.columns), jnp.float32),
+        ),
+        in_specs=[away, away, held, held, away, away, away, away, away, away],
+        out_specs=(held, held),
+        scratch_shapes=[
+            pltpu.VMEM((rows, channels), bf),
+            pltpu.VMEM((tiles, depth, TILE), bf),
+            pltpu.VMEM(w_query.shape, bf),
+            pltpu.VMEM(w_key.shape, bf),
+            pltpu.VMEM(w_value.shape, bf),
+            pltpu.VMEM(w_out.shape, bf),
+            pltpu.VMEM((tokens, width), bf),
+            pltpu.VMEM((tokens, 2 * KEY), jnp.float32),
+            pltpu.SemaphoreType.DMA((8 + tiles,)),
+            pltpu.VMEM((2, EDGE, channels), bf),
+            pltpu.SemaphoreType.DMA((4,)),
+            pltpu.VMEM((channels // 128, rows + 2 * EDGE, 128), jnp.float32),
+            pltpu.VMEM((rows, depth), bf),
+            pltpu.VMEM((tokens, width), bf),
+            pltpu.VMEM((tokens, width), bf),
+            pltpu.VMEM((w_query.shape[1] // KEY, tokens, KEY), bf),
+            pltpu.VMEM((seq, tokens, KEY), bf),
+            pltpu.VMEM((seq, tokens, VAL), bf),
+            pltpu.SemaphoreType.DMA((4 * max(seq - 1, 1),)),
+        ]
+        + plan.scratch(),
+        compiler_params=pltpu.CompilerParams(
+            collective_id=1, has_side_effects=True, vmem_limit_bytes=60 * 2**20
+        ),
+        name="section",
+    )(
+        inputs,
+        kernel_weight.reshape(depth, width),
+        conv_bias[None],
+        norm_gain[None],
+        w_query,
+        w_key,
+        w_value,
+        w_out,
+        upstream,
+        turn_table(tokens * seq),
+    )
+    return mixed[None], gradient
 
 
 def local(x_in, kernel_weight, conv_bias, norm_gain, w_query, w_key, w_value, w_out, cotangent):
@@ -430,7 +741,7 @@
 
 def solution(mesh):
     return jax.shard_map(
-        local,
+        section if mesh.shape["head"] == 1 else local,
         mesh=mesh,
         in_specs=(
             P(("groups", "dp"), "seq", None),

time: 144 us -> 91.1 us (0.63)
  matrix products: 41.7 us -> 0 us
  Pallas kernels: 48.3 us -> 80.1 us
  blocking collectives: 19 us -> 0 us
  other arithmetic: 13.2 us -> 0 us
  starting transfers between devices: 6.35 us -> 0 us
  local copies, waits for them, and re-layouts: 14.3 us -> 10.1 us
    dot_general x11 -> x0, matrix products: 41.7 us -> none  [the longest x3 14.1 us: local(): jnp.dot(padded_rows[kernel_tap_index * DILATION_STEP:kernel_tap_index * D...]
    pallas_call x1, Pallas kernels: 48.3 us -> 80.1 us  [section(): pl.pallas_call(functools.partial(section_kernel, plan), out_shape=(jax.Sh...]
    all_gather x1 -> x0, blocking collectives: 19 us -> none  [local(): lax.all_gather(jnp.concatenate([key_rows, value_rows], axis=1), ('seq', '...]
    reshape x2 -> x0, local copies, waits for them, and re-layouts: 6.79 us -> none  [the longest x1 4.5 us: local(): activated.reshape(padded_row_count // 2, 2, -1)]
    ppermute x2 -> x0, starting transfers between devices: 6.35 us -> none  [the longest x1 5.05 us: padded(): lax.ppermute(tail, axis, [(i, (i + 1) % count) for i in range(ends)])]
    reduce_max x1 -> x0, other arithmetic: 6.11 us -> none  [local(): jnp.max(activated.reshape(padded_row_count // 2, 2, -1), axis=1)]
    unnamed x22 -> x3, local copies, waits for them, and re-layouts: 2.88 us -> 7.5 us
    reduce_sum x3 -> x0, other arithmetic: 2.75 us -> none  [the longest x2 1.39 us: one_block(): running_sum = running_sum * rescale + jnp.sum(weights, axis=-1)]
  transfers between devices with their start and end apart: 2 -> 0, of which waited for: 0 -> 0; matrix products, arithmetic and copies ran while one was open for 6% -> 0% of each run, Pallas kernels for 0% -> 0%
where the time goes in v2:
time: 91.1 us; the launch traced here: 90.8 us
  Pallas kernels  80.1 us (88%)
  local copies, waits for them, and re-layouts  10.1 us (11%)
    pallas_call x1, Pallas kernels, section(): pl.pallas_call(functools.partial(section_kernel, plan), out_shape=(jax.Sh...  80.1 us
    unnamed x3, local copies, waits for them, and re-layouts  7.5 us

profile of v2, /device:TPU:0, one launch (start us, length us, event | category | flops | bytes accessed | tf_op | source)
XLA Modules:
  0.0 90.8 jit_solution(15204876422417438686)
XLA Ops:
  0.6 1.3 %broadcast_in_dim.9.refs_2_ = f32[1,1536]{1,0:T(1,128)} reshape(f32[1536]{0:T(1024)} %param.12) | data formatting | bytes 12288 | tf_op jit(solution)/shard_map/broadcast_in_dim | solution.py:653
  1.9 1.3 %broadcast_in_dim.10.refs_3_ = f32[1,1536]{1,0:T(1,128)} reshape(f32[1536]{0:T(1024)} %param.13) | data formatting | bytes 12288 | tf_op jit(solution)/shard_map/broadcast_in_dim | solution.py:654
  3.2 2.2 %copy.12.refs_6_ = bf16[1536,192]{1,0:T(8,128)(2,1)} copy(bf16[1536,192]{0,1:T(8,128)(2,1)} %param.16) | data formatting | bytes 1179648 | tf_op args[6]
  5.4 80.1 %section.1 = (bf16[256,1536]{1,0:T(8,128)(2,1)}, f32[384,1536]{1,0:T(8,128)}) custom-call(bf16[512,768]{1,0:T(8,128)(2,1)} %bitcast.5, bf16[2304,1536]{1,0:T(8,128)(2,1)} %bitcast.4, f32[1,1536]{1,0:T(1,128)} %broadcast_in_dim.9.refs_2_, f32[1,1536]{1,0:T(1,128)} %broadcast_in_dim.10.refs_3_, bf16[1536,1024]{1,0:T(8,128)(2,1)} %refs_4_.1, ...), custom_call_target="tpu_custom_call" | custom-call | tf_op jit(solution)/shard_map/section/pallas_call | solution.py:616
  85.5 2.1 %copy.15 = bf16[1,256,1536]{2,1,0:T(8,128)(2,1)} copy(bf16[1,256,1536]{2,1,0:T(8,128)(2,1)} %bitcast.7) | data formatting | bytes 1572864
  87.6 3.2 %copy.16 = f32[384,1536]{1,0:T(8,128)} copy(f32[384,1536]{1,0:T(8,128)} %get-tuple-element.9) | data formatting | bytes 4718592

commit v3 on v2

--- a/solution.py
+++ b/solution.py
@@ -99,18 +99,21 @@
         self.dp, self.seq = dp, seq
         self.levels = dp.bit_length() - 1
         self.block = width // dp
-        self.rows = 128 if self.block % 128 == 0 else self.block
+        self.rows = 64 if self.block % 64 == 0 else self.block
         self.pieces = self.block // self.rows
         self.chunk = 2 * VAL
         self.chunks = columns // self.chunk
         self.units = self.chunks * self.pieces
+        self.gap = 4
 
     def scratch(self):
         tile = (self.rows, self.chunk)
+        self.slots = self.gap * self.levels + 1
         shapes = [
-            pltpu.VMEM((self.width, self.tokens), jnp.bfloat16),
+            pltpu.VMEM((self.pieces, self.dp * self.rows, self.tokens), jnp.bfloat16),
             pltpu.VMEM((self.chunks, self.tokens, self.chunk), jnp.bfloat16),
             pltpu.VMEM((self.units,) + tile, jnp.float32),
+            pltpu.VMEM((self.slots, self.dp * self.rows, self.chunk), jnp.float32),
         ]
         sends = self.levels + 2
         for level in range(self.levels):
@@ -121,29 +124,30 @@
         return shapes
 
 
+def turn_over(plan, cot_ref, cot_t):
+    for piece in range(plan.pieces):
+        for p in range(plan.dp):
+            start = p * plan.block + piece * plan.rows
+            cot_t[piece, p * plan.rows : (p + 1) * plan.rows, :] = jnp.transpose(
+                cot_ref[:, start : start + plan.rows]
+            )
+
+
 def gradient_loop(plan, refs, out_ref, produce=None, least=0):
-    cot_t, att, own = refs[:3]
+    cot_t, att, own, products = refs[:4]
+    refs = refs[1:]
     levels, units = plan.levels, plan.units
     pairs = refs[3 : 3 + 2 * levels]
     ahead_out, ahead_in, back_out, back_in = refs[3 + 2 * levels : 7 + 2 * levels]
     sems = refs[7 + 2 * levels :]
     d = lax.axis_index("dp")
     s = lax.axis_index("seq")
-    gap = 2
+    gap = plan.gap
     last = plan.seq - 1
 
-    def product(unit, p):
-        start = pl.multiple_of(
-            p * plan.block + (unit % plan.pieces) * plan.rows, plan.rows
-        )
-        return jnp.dot(
-            cot_t[pl.ds(start, plan.rows), :],
-            att[unit // plan.pieces],
-            preferred_element_type=jnp.float32,
-        )
-
     def summed(unit, p, level):
-        value = product(unit, p)
+        start = pl.multiple_of(p * plan.rows, plan.rows)
+        value = products[unit % plan.slots, pl.ds(start, plan.rows), :]
         for done in range(level):
             value = value + pairs[2 * done + 1][unit, p // (2 << done)].astype(jnp.float32)
         return value
@@ -184,7 +188,13 @@
 
             @pl.when(within(unit))
             def _(unit=unit, level=level):
-                if level > 0:
+                if level == 0:
+                    products[unit % plan.slots] = jnp.dot(
+                        cot_t[unit % plan.pieces],
+                        att[unit // plan.pieces],
+                        preferred_element_type=jnp.float32,
+                    )
+                else:
                     level_copy(unit, level - 1).wait_recv()
                 step = 1 << level
                 base = d % step + (1 - (d // step) % 2) * step
@@ -200,6 +210,12 @@
         def _():
             if levels > 0:
                 level_copy(unit, levels - 1).wait_recv()
+            else:
+                products[unit % plan.slots] = jnp.dot(
+                    cot_t[unit % plan.pieces],
+                    att[unit // plan.pieces],
+                    preferred_element_type=jnp.float32,
+                )
             own[unit] = summed(unit, d, levels)
 
         if last > 0:
@@ -329,7 +345,7 @@
 
 def gradient_kernel(plan, cot_ref, att_ref, out_ref, *refs):
     greet(plan)
-    refs[0][...] = jnp.transpose(cot_ref[...])
+    turn_over(plan, cot_ref, refs[0])
     for c in range(plan.chunks):
         refs[1][c] = att_ref[:, c * plan.chunk : (c + 1) * plan.chunk]
     gradient_loop(plan, refs, out_ref)
@@ -354,30 +370,18 @@
     )(upstream, attended)
 
 
-def meet(plan):
-    barrier = pltpu.get_barrier_semaphore()
-    d = lax.axis_index("dp")
-    s = lax.axis_index("seq")
-    for level in range(plan.levels):
-        step = 1 << level
-        signal_to(barrier, {"dp": d + (1 - 2 * ((d // step) % 2)) * step})
-    for j in range(1, plan.seq):
-        signal_to(barrier, {"seq": (s + j) % plan.seq})
-    pl.semaphore_wait(barrier, plan.levels + plan.seq - 1)
-
-
 EDGE = 16
 TILE = 256
 
 
 def section_kernel(plan, *refs):
-    (x_hbm, conv_hbm, bias, gain, query_hbm, key_hbm, value_hbm, out_hbm, cot_hbm, turn_hbm) = refs[:10]
+    (x_hbm, conv_hbm, bias_in, gain_in, query_hbm, key_hbm, value_hbm, out_hbm, cot_hbm, turn_hbm) = refs[:10]
     mixed, grad_out = refs[10:12]
     (
         x_rows, conv_w, query_w, key_w, value_w, out_w, cot, turn, fetched,
-        edges, edge_sems, spread, stacked, pooled, normed, queries, keys, values, kv_sems,
-    ) = refs[12:31]
-    gradient_refs = refs[31:]
+        edges, edge_sems, spread, stacked, pooled, normed, queries, kv, values, kv_sems, bias, gain,
+    ) = refs[12:33]
+    gradient_refs = refs[33:]
     cot_t, att = gradient_refs[:2]
     tokens, rows = plan.tokens, 2 * plan.tokens
     s = lax.axis_index("seq")
@@ -407,7 +411,9 @@
     for fetch in (key_fetch, value_fetch, turn_fetch, query_fetch, cot_fetch, out_fetch):
         fetch.start()
 
-    meet(plan)
+    bias[...] = bias_in[...].reshape(bias.shape)
+    gain[...] = gain_in[...].reshape(gain.shape)
+    greet(plan)
 
     def edge_ahead():
         return remote(
@@ -436,32 +442,40 @@
     for j in range(blocks):
         spread[j, EDGE : EDGE + rows, :] = x_rows[:, j * 128 : (j + 1) * 128].astype(jnp.float32)
     blank = jnp.zeros((EDGE, 128), jnp.float32)
-
-    def put_edge(which, start, there):
-        @pl.when(there)
-        def _():
-            if last > 0:
-                (edge_ahead if which == 0 else edge_back)().wait_recv()
-                for j in range(blocks):
-                    spread[j, start : start + EDGE, :] = edges[
-                        which, :, j * 128 : (j + 1) * 128
-                    ].astype(jnp.float32)
-
-        @pl.when(jnp.logical_not(there))
-        def _():
+    for j in range(blocks):
+        spread[j, :EDGE, :] = blank
+        spread[j, EDGE + rows :, :] = blank
+
+    def stack(tap, first, count):
+        for parity in range(2):
             for j in range(blocks):
-                spread[j, start : start + EDGE, :] = blank
-
-    put_edge(0, 0, s > 0)
-    put_edge(1, EDGE + rows, s < last)
-    for parity in range(2):
-        for tap in range(taps):
-            for j in range(blocks):
-                start = EDGE + parity + DILATION_STEP * (tap - 1)
+                start = EDGE + parity + DILATION_STEP * (tap - 1) + 2 * first
                 lane = tap * channels + j * 128
-                stacked[parity * tokens : (parity + 1) * tokens, lane : lane + 128] = spread[
-                    j, pl.ds(start, tokens, stride=2), :
+                row = parity * tokens + first
+                stacked[row : row + count, lane : lane + 128] = spread[
+                    j, pl.ds(start, count, stride=2), :
                 ].astype(jnp.bfloat16)
+
+    for tap in range(taps):
+        stack(tap, 0, tokens)
+
+    def put_edge(which, start, tap, first):
+        (edge_ahead if which == 0 else edge_back)().wait_recv()
+        for j in range(blocks):
+            spread[j, start : start + EDGE, :] = edges[which, :, j * 128 : (j + 1) * 128].astype(
+                jnp.float32
+            )
+        stack(tap, first, EDGE)
+
+    if last > 0:
+
+        @pl.when(s > 0)
+        def _():
+            put_edge(0, 0, 0, 0)
+
+        @pl.when(s < last)
+        def _():
+            put_edge(1, EDGE + rows, taps - 1, tokens - EDGE)
 
     def conv_tile(n, carry):
         conv_fetch(n).wait()
@@ -499,24 +513,40 @@
             vectors * turn[:, :KEY] + pltpu.roll(vectors, KEY // 2, 1) * turn[:, KEY:]
         ).astype(jnp.bfloat16)
 
-    keys[s] = turned(jnp.dot(normed[...], key_w[...], preferred_element_type=jnp.float32))
-    values[s] = jnp.dot(normed[...], value_w[...], preferred_element_type=jnp.float32).astype(
-        jnp.bfloat16
-    )
-
-    def kv_copies(owner, j, peer):
-        at = 4 * (j - 1)
-        return (
-            remote(keys.at[owner], keys.at[owner], kv_sems.at[at], kv_sems.at[at + 1], {"seq": peer}),
-            remote(
-                values.at[owner], values.at[owner], kv_sems.at[at + 2], kv_sems.at[at + 3],
-                {"seq": peer},
-            ),
-        )
-
-    for j in range(1, plan.seq):
-        for copy in kv_copies(s, j, (s + j) % plan.seq):
-            copy.start()
+    half = tokens // 2
+    kv[s, :tokens, :] = turned(
+        jnp.dot(normed[...], key_w[...], preferred_element_type=jnp.float32)
+    )
+    own_values = lax.dot_general(
+        normed[...], value_w[...], (((1,), (1,)), ((), ())), preferred_element_type=jnp.float32
+    )
+    kv[s, tokens : 2 * tokens, :] = own_values[:, :128].astype(jnp.bfloat16)
+    kv[s, 2 * tokens :, :] = jnp.concatenate(
+        [own_values[:half, 128:], own_values[half:, 128:]], axis=1
+    ).astype(jnp.bfloat16)
+    split = 5 * tokens // 4
+
+    def kv_copy(way, hop, h):
+        owner = s - hop if way == 0 else s + hop
+        owner = jnp.clip(owner, 0, last)
+        at = ((way * last + hop) * 2 + h) * 2
+        block = kv.at[owner, pl.ds(h * split, split)]
+        return remote(
+            block, block, kv_sems.at[at], kv_sems.at[at + 1],
+            {"seq": s + 1 if way == 0 else s - 1},
+        )
+
+    def kv_sent(way, hop):
+        if way == 0:
+            return jnp.logical_and(s >= hop, s < last)
+        return jnp.logical_and(s + hop <= last, s > 0)
+
+    for way in range(2) if last > 0 else ():
+
+        @pl.when(kv_sent(way, 0))
+        def _(way=way):
+            kv_copy(way, 0, 0).start()
+            kv_copy(way, 0, 1).start()
 
     query_fetch.wait()
 
@@ -532,17 +562,31 @@
 
     lax.fori_loop(0, plan.chunks, query_pair, 0)
     cot_fetch.wait()
-    cot_t[...] = jnp.transpose(cot[...])
+    turn_over(plan, cot, cot_t)
     out_fetch.wait()
-    for j in range(1, plan.seq):
-        owner = (s + plan.seq - j) % plan.seq
-        for copy in kv_copies(owner, j, (s + j) % plan.seq):
-            copy.wait_recv()
+    for hop in range(last):
+        for h in range(2):
+            for way in range(2):
+                got = s > hop if way == 0 else s + hop < last
+
+                @pl.when(got)
+                def _(hop=hop, h=h, way=way):
+                    kv_copy(way, hop, h).wait_recv()
+
+                    @pl.when(s < last if way == 0 else s > 0)
+                    def _():
+                        if hop + 1 < last:
+                            kv_copy(way, hop + 1, h).start()
+
+    for j in range(plan.seq):
+        values[j, :, :128] = kv[j, tokens : 2 * tokens, :]
+        values[j, :half, 128:] = kv[j, 2 * tokens :, : VAL - 128]
+        values[j, half:, 128:] = kv[j, 2 * tokens :, VAL - 128 :]
 
     def attend_head(h):
         scores = lax.dot_general(
             queries[h],
-            keys[...].reshape(plan.seq * tokens, KEY),
+            kv[:, :tokens, :].reshape(plan.seq * tokens, KEY),
             (((1,), (1,)), ((), ())),
             preferred_element_type=jnp.float32,
         )
@@ -578,9 +622,14 @@
 
     gradient_loop(plan, gradient_refs, grad_out, produce, plan.units + tiles)
 
-    for j in range(1, plan.seq):
-        for copy in kv_copies(s, j, (s + j) % plan.seq):
-            copy.wait_send()
+    for hop in range(last):
+        for way in range(2):
+
+            @pl.when(kv_sent(way, hop))
+            def _(hop=hop, way=way):
+                kv_copy(way, hop, 0).wait_send()
+                kv_copy(way, hop, 1).wait_send()
+
     if last > 0:
 
         @pl.when(s < last)
@@ -626,7 +675,7 @@
             pltpu.VMEM((tiles, depth, TILE), bf),
             pltpu.VMEM(w_query.shape, bf),
             pltpu.VMEM(w_key.shape, bf),
-            pltpu.VMEM(w_value.shape, bf),
+            pltpu.VMEM(w_value.shape[::-1], bf),
             pltpu.VMEM(w_out.shape, bf),
             pltpu.VMEM((tokens, width), bf),
             pltpu.VMEM((tokens, 2 * KEY), jnp.float32),
@@ -638,9 +687,11 @@
             pltpu.VMEM((tokens, width), bf),
             pltpu.VMEM((tokens, width), bf),
             pltpu.VMEM((w_query.shape[1] // KEY, tokens, KEY), bf),
-            pltpu.VMEM((seq, tokens, KEY), bf),
+            pltpu.VMEM((seq, 5 * tokens // 2, KEY), bf),
             pltpu.VMEM((seq, tokens, VAL), bf),
-            pltpu.SemaphoreType.DMA((4 * max(seq - 1, 1),)),
+            pltpu.SemaphoreType.DMA((8 * max(seq - 1, 1),)),
+            pltpu.VMEM((1, width), jnp.float32),
+            pltpu.VMEM((1, width), jnp.float32),
         ]
         + plan.scratch(),
         compiler_params=pltpu.CompilerParams(
@@ -650,11 +701,11 @@
     )(
         inputs,
         kernel_weight.reshape(depth, width),
-        conv_bias[None],
-        norm_gain[None],
+        conv_bias,
+        norm_gain,
         w_query,
         w_key,
-        w_value,
+        jnp.transpose(w_value),
         w_out,
         upstream,
         turn_table(tokens * seq),

time: 91.1 us -> 78.5 us (0.86)
  Pallas kernels: 80.1 us -> 72.3 us
  local copies, waits for them, and re-layouts: 10.1 us -> 5.28 us
    pallas_call x1, Pallas kernels: 80.1 us -> 72.3 us  [section(): pl.pallas_call(functools.partial(section_kernel, plan), out_shape=(jax.Sh...]
    broadcast_in_dim x2 -> x0, local copies, waits for them, and re-layouts: 2.58 us -> none  [the longest x1 1.3 us: section(): conv_bias[None]]
    unnamed x3 -> x2, local copies, waits for them, and re-layouts: 7.5 us -> 5.28 us
where the time goes in v3:
time: 78.5 us; the launch traced here: 78.3 us
  Pallas kernels  72.3 us (92%)
  local copies, waits for them, and re-layouts  5.28 us (7%)
    pallas_call x1, Pallas kernels, section(): pl.pallas_call(functools.partial(section_kernel, plan), out_shape=(jax.Sh...  72.3 us
    unnamed x2, local copies, waits for them, and re-layouts  5.28 us

profile of v3, /device:TPU:0, one launch (start us, length us, event | category | flops | bytes accessed | tf_op | source)
XLA Modules:
  0.0 78.3 jit_solution(16569322021260442866)
XLA Ops:
  0.6 72.3 %section.1 = (bf16[256,1536]{1,0:T(8,128)(2,1)}, f32[384,1536]{1,0:T(8,128)}) custom-call(bf16[512,768]{1,0:T(8,128)(2,1)} %bitcast.7, bf16[2304,1536]{1,0:T(8,128)(2,1)} %bitcast.5, f32[1536]{0:T(1024)} %refs_2_.1, f32[1536]{0:T(1024)} %refs_3_.1, bf16[1536,1024]{1,0:T(8,128)(2,1)} %refs_4_.1, bf16[1536,128]{1,0:T(8,128)(2,1)} %refs_5_.1, ...), custom_call_target="tpu_custom_call" | custom-call | tf_op jit(solution)/shard_map/section/pallas_call | solution.py:665
  73.0 2.1 %copy.14 = bf16[1,256,1536]{2,1,0:T(8,128)(2,1)} copy(bf16[1,256,1536]{2,1,0:T(8,128)(2,1)} %bitcast.6) | data formatting | bytes 1572864
  75.0 3.2 %copy.15 = f32[384,1536]{1,0:T(8,128)} copy(f32[384,1536]{1,0:T(8,128)} %get-tuple-element.9) | data formatting | bytes 4718592

commit v4 on v3

--- a/solution.py
+++ b/solution.py
@@ -260,7 +260,7 @@
         def store(value):
             row = pl.multiple_of((ready % plan.pieces) * plan.rows, plan.rows)
             column = pl.multiple_of((ready // plan.pieces) * plan.chunk, plan.chunk)
-            out_ref[pl.ds(row, plan.rows), pl.ds(column, plan.chunk)] = value
+            out_ref[pl.ds(row, plan.rows), pl.ds(column, plan.chunk)] = value.astype(out_ref.dtype)
 
         if last == 0:
 
@@ -666,7 +666,7 @@
         functools.partial(section_kernel, plan),
         out_shape=(
             jax.ShapeDtypeStruct((tokens, width), bf),
-            jax.ShapeDtypeStruct((plan.block, plan.columns), jnp.float32),
+            jax.ShapeDtypeStruct((plan.block, plan.columns), bf),
         ),
         in_specs=[away, away, held, held, away, away, away, away, away, away],
         out_specs=(held, held),
@@ -710,7 +710,7 @@
         upstream,
         turn_table(tokens * seq),
     )
-    return mixed[None], gradient
+    return mixed[None], gradient.astype(jnp.float32)
 
 
 def local(x_in, kernel_weight, conv_bias, norm_gain, w_query, w_key, w_value, w_out, cotangent):

time: 78.5 us -> 76.8 us (0.978)
  local copies, waits for them, and re-layouts: 5.28 us -> 0.88 us
  other arithmetic: 0 us -> 3.04 us
    unnamed x2 -> x3, local copies, waits for them, and re-layouts: 5.28 us -> 0.88 us
    convert_element_type x0 -> x1, other arithmetic: none -> 3.04 us  [section(): return (mixed[None], gradient.astype(jnp.float32))]
where the time goes in v4:
time: 76.8 us; the launch traced here: 76.5 us
  Pallas kernels  71.9 us (94%)
  other arithmetic  3.04 us (4%)
  local copies, waits for them, and re-layouts  0.88 us (1%)
    pallas_call x1, Pallas kernels, section(): pl.pallas_call(functools.partial(section_kernel, plan), out_shape=(jax.Sh...  71.9 us
    convert_element_type x1, other arithmetic, section(): return (mixed[None], gradient.astype(jnp.float32))  3.04 us

profile of v4, /device:TPU:0, one launch (start us, length us, event | category | flops | bytes accessed | tf_op | source)
XLA Modules:
  0.0 76.5 jit_solution(6743416446666165399)
XLA Ops:
  0.6 71.9 %section.1 = (bf16[256,1536]{1,0:T(8,128)(2,1)}, bf16[384,1536]{1,0:T(8,128)(2,1)}) custom-call(bf16[512,768]{1,0:T(8,128)(2,1)} %bitcast.7, bf16[2304,1536]{1,0:T(8,128)(2,1)} %bitcast.5, f32[1536]{0:T(1024)} %refs_2_.1, f32[1536]{0:T(1024)} %refs_3_.1, bf16[1536,1024]{1,0:T(8,128)(2,1)} %refs_4_.1, bf16[1536,128]{1,0:T(8,128)(2,1)} %refs_5_.1, ...), custom_call_target="tpu_custom_call" | custom-call | tf_op jit(solution)/shard_map/section/pallas_call | solution.py:665
  72.6 0.0 copy-start
  72.6 3.0 %convert_element_type.3 = f32[384,1536]{1,0:T(8,128)} convert(bf16[384,1536]{1,0:T(8,128)(2,1)} %get-tuple-element.5) | non-fusion elementwise | flops 589824 | bytes 3538944 | tf_op jit(solution)/shard_map/convert_element_type | solution.py:713
  75.6 0.0 copy-done
  75.6 0.9 %copy.13 = bf16[1,256,1536]{2,1,0:T(8,128)(2,1)} copy(bf16[1,256,1536]{2,1,0:T(8,128)(2,1)S(1)} %bitcast.6) | data formatting | bytes 1572864
Async XLA Ops:
  72.6 3.1 %copy-start = (bf16[256,1536]{1,0:T(8,128)(2,1)S(1)}, bf16[256,1536]{1,0:T(8,128)(2,1)}, u32[]{:S(2)}) copy-start(bf16[256,1536]{1,0:T(8,128)(2,1)} %get-tuple-element.4) | copy-start | bytes 2359300
